TPU v7x, 128 devices: a whole 4x4x4 slice. The times are simulated.
128 devices in a mesh: stream: 64 (over z, y, x), seq: 2 (over core).
Axes of the slice: x: 4, y: 4, z: 4, core: 2. Of those that a mesh axis runs over, the one named last changes fastest.
Arguments:
- head_inputs: bfloat16 [64, 3072, 1536], P('stream', 'seq'), may hold values from -6 to 6
- state_maps: bfloat16 [64, 3072, 256], P('stream', 'seq'), may hold values from -2.1 to 2.1
- step_logits: float32 [64, 24, 3072], P('stream', None, 'seq'), may hold values from -3 to 5.5
- log_rates: float32 [24], replicated, may hold values from -7 to 0
- step_bias: float32 [24], replicated, may hold values from -6 to -2
- skip_gain: float32 [24], replicated, may hold values from 0.25 to 1.75
- old_states: float32 [64, 24, 64, 128], P('stream', 'seq'), may hold values from -6 to 6
- old_owner: int32 [64], replicated, may hold values from 0 to 63, as said below
- doc_starts: int32 [64, 2], P('stream'), may hold values from 0 to 3071
- grad_output: bfloat16 [64, 3072, 1536], P('stream', 'seq'), may hold values from -6 to 6
Outputs:
- layer_out: bfloat16 [64, 3072, 1536], P('stream', 'seq')
- grad_inputs: bfloat16 [64, 3072, 1536], P('stream', 'seq')
- grad_maps: bfloat16 [64, 3072, 256], P('stream', 'seq')
- grad_logits: float32 [64, 24, 3072], P('stream', None, 'seq')
- grad_rates: float32 [24], replicated
- grad_bias: float32 [24], replicated
- grad_skip: float32 [24], replicated
Inputs may be any that keep to these rules, and one draw needn't show every extreme that they name: A permutation of the 64 stream indices: new stream s continues old stream old_owner[s]. `doc_starts`: positions in a stream's segment where a document starts and the state is cleared; entries may repeat.
All inputs are finite; a program needn't handle non-finite values.
Results may differ from a plain program's by a relative error of at most 0.013.
Values sent between devices are 32-bit elements; how exact they have to be, the bound alone decides.
No kernel may reach another device: no remote copies, remote signals or barrier semaphores. Data moves between devices by JAX's collectives and lax.ppermute only.
A program may use at most 192 MiB of HBM per device.

v0:
```python
import jax
import jax.numpy as jnp
from jax import lax
from jax.sharding import PartitionSpec as P

GROUP = 256


def shifted_2(shard, axis, by):
    size = lax.axis_size(axis)
    pairs = [(i, i + by) for i in range(size) if 0 <= i + by < size]
    return lax.ppermute(shard, axis, pairs)


def decay_terms(logits_part, flags_part, log_rates, step_bias):
    step_size = jax.nn.softplus(logits_part + step_bias[:, None])
    cum_decay = jnp.cumsum(-step_size * jnp.exp(log_rates)[:, None], axis=-1)
    doc_index = jnp.cumsum(flags_part, axis=-1)
    return (step_size, cum_decay, doc_index)


def group_states(inputs_c, maps_c, logits_c, flags_c, log_rates, step_bias):
    step_size, cum_decay, doc_index = decay_terms(logits_c, flags_c, log_rates, step_bias)
    state_n = maps_c.shape[-1] // 2
    b_part = maps_c[:, :, :state_n].astype(jnp.float32)
    same_doc = doc_index == doc_index[:, -1:]
    weight = (
        jnp.where(same_doc[:, None, :], jnp.exp(cum_decay[:, :, -1:] - cum_decay), 0.0) * step_size
    )
    b_weighted = (weight[:, :, :, None] * b_part[:, None, :, :]).astype(jnp.bfloat16)
    states = jnp.einsum("cjhp,chjn->chpn", inputs_c, b_weighted, preferred_element_type=jnp.float32)
    decays = jnp.where(doc_index[:, -1:] == 0, jnp.exp(cum_decay[:, :, -1]), 0.0)
    return (states, decays)


def group_inputs(start_state, states, decays):

    def advance(carry, members):
        group_state, group_decay = members
        return (group_decay[:, None, None] * carry + group_state, carry)

    return lax.scan(advance, start_state, (states, decays))


def one_group(inputs_q, maps_q, logits_q, flags_q, starts_q, log_rates, step_bias, skip_gain):
    step_size, cum_decay, doc_index = decay_terms(logits_q, flags_q, log_rates, step_bias)
    state_n = maps_q.shape[-1] // 2
    b_part = maps_q[:, :state_n]
    c_part = maps_q[:, state_n:]
    scores = jnp.dot(c_part, b_part.T, preferred_element_type=jnp.float32)
    position = jnp.arange(maps_q.shape[0])
    visible = (position[None, :] <= position[:, None]) & (doc_index[None, :] == doc_index[:, None])
    log_gaps = jnp.where(visible[None], cum_decay[:, :, None] - cum_decay[:, None, :], -jnp.inf)
    mixing = (scores[None] * jnp.exp(log_gaps) * step_size[:, None, :]).astype(jnp.bfloat16)
    local_part = jnp.einsum("hij,jhp->ihp", mixing, inputs_q, preferred_element_type=jnp.float32)
    inflow = jnp.where(doc_index[None, :] == 0, jnp.exp(cum_decay), 0.0)
    carried = jnp.einsum(
        "in,hpn->ihp", c_part.astype(jnp.float32), starts_q, precision=lax.Precision.HIGHEST
    )
    summed = (
        local_part
        + carried * inflow.T[:, :, None]
        + skip_gain[None, :, None] * inputs_q.astype(jnp.float32)
    )
    return summed.reshape(inputs_q.shape[0], -1).astype(jnp.bfloat16)


def outputs(inputs_c, maps_c, logits_c, flags_c, log_rates, step_bias, skip_gain, starts_c):

    def per_group(carry, members):
        inputs_q, maps_q, logits_q, flags_q, starts_q = members
        return (
            carry,
            jax.checkpoint(one_group)(
                inputs_q, maps_q, logits_q, flags_q, starts_q, log_rates, step_bias, skip_gain
            ),
        )

    _, result = lax.scan(per_group, 0, (inputs_c, maps_c, logits_c, flags_c, starts_c))
    return result


def shards(
    head_inputs,
    state_maps,
    step_logits,
    log_rates,
    step_bias,
    skip_gain,
    old_states,
    old_owner,
    doc_starts,
    grad_output,
):
    length = head_inputs.shape[1]
    head_count = step_logits.shape[1]
    head_dim = old_states.shape[2]
    state_n = old_states.shape[3]
    groups = length // GROUP
    seq_index = lax.axis_index("seq")
    stream_index = lax.axis_index("stream")
    position = seq_index * length + lax.iota(jnp.int32, length)
    reset_flags = jnp.any(doc_starts[0][:, None] == position[None, :], axis=0).astype(jnp.int32)
    gathered = lax.all_gather(old_states, "stream", axis=0, tiled=True)
    own_block = lax.dynamic_index_in_dim(gathered, old_owner[stream_index], 0, keepdims=False)
    start_state = lax.all_gather(own_block, "seq", axis=0, tiled=True)
    inputs_c = head_inputs[0].reshape(groups, GROUP, head_count, head_dim)
    maps_c = state_maps[0].reshape(groups, GROUP, 2 * state_n)
    logits_c = step_logits[0].reshape(head_count, groups, GROUP).transpose(1, 0, 2)
    flags_c = reset_flags.reshape(groups, GROUP)

    def state_part(inputs_c, maps_c, logits_c, log_rates, step_bias):
        return group_states(inputs_c, maps_c, logits_c, flags_c, log_rates, step_bias)

    (states, decays), pull_states = jax.vjp(
        state_part, inputs_c, maps_c, logits_c, log_rates, step_bias
    )
    empty_state = jnp.zeros((head_count, head_dim, state_n), jnp.float32)
    local_state, _ = group_inputs(empty_state, states, decays)
    shard_decay = jnp.prod(decays, axis=0)
    is_first = seq_index == 0

    def forward_turn(counter, entering):
        leaving = shard_decay[:, None, None] * entering + local_state
        shifted = shifted_2(leaving, "seq", 1)
        return jnp.where(is_first, start_state, shifted)

    entry_state = lax.fori_loop(0, lax.axis_size("seq") - 1, forward_turn, start_state)
    (exit_state, starts_c), pull_inputs = jax.vjp(group_inputs, entry_state, states, decays)

    def output_part(inputs_c, maps_c, logits_c, log_rates, step_bias, skip_gain, starts_c):
        return outputs(
            inputs_c, maps_c, logits_c, flags_c, log_rates, step_bias, skip_gain, starts_c
        )

    result, pull_output = jax.vjp(
        output_part, inputs_c, maps_c, logits_c, log_rates, step_bias, skip_gain, starts_c
    )
    grads_c = grad_output[0].reshape(groups, GROUP, head_count * head_dim)
    in_first, maps_first, logits_first, rates_first, bias_first, skip_total, grad_starts = (
        pull_output(grads_c)
    )
    from_output = pull_inputs((jnp.zeros_like(exit_state), grad_starts))[0]

    def backward_turn(counter, leaving_grad):
        entering_grad = shard_decay[:, None, None] * leaving_grad + from_output
        return shifted_2(entering_grad, "seq", -1)

    exit_grad = lax.fori_loop(0, lax.axis_size("seq") - 1, backward_turn, empty_state)
    _, grad_states, grad_decays = pull_inputs((exit_grad, grad_starts))
    in_second, maps_second, logits_second, rates_second, bias_second = pull_states(
        (grad_states, grad_decays)
    )
    rates_total, bias_total, skip_sum = lax.psum(
        (rates_first + rates_second, bias_first + bias_second, skip_total), ("stream", "seq")
    )
    grad_logits = (logits_first + logits_second).transpose(1, 0, 2).reshape(1, head_count, length)
    return (
        result.reshape(1, length, -1),
        (in_first + in_second).reshape(1, length, -1),
        (maps_first + maps_second).reshape(1, length, -1),
        grad_logits,
        rates_total,
        bias_total,
        skip_sum,
    )


def solution(mesh):
    return jax.shard_map(
        shards,
        mesh=mesh,
        in_specs=(
            P("stream", "seq", None),
            P("stream", "seq", None),
            P("stream", None, "seq"),
            P(),
            P(),
            P(),
            P("stream", "seq", None, None),
            P(),
            P("stream", None),
            P("stream", "seq", None),
        ),
        out_specs=(
            P("stream", "seq", None),
            P("stream", "seq", None),
            P("stream", "seq", None),
            P("stream", None, "seq"),
            P(),
            P(),
            P(),
        ),
        check_vma=False,
    )
```

profile of v0, /device:TPU:1, one launch (start us, length us, event | category | flops | bytes accessed | tf_op | source)
XLA Modules:
  0.0 601.4 jit_solution(6530939128043399756)
XLA Ops:
  11.3 1.8 reduce-window.126
  16.1 3.5 reduce-window.128
  21.2 12.9 %reshape.634 = bf16[6,256,24,64]{3,2,1,0:T(8,128)(2,1)} reshape(bf16[1,1536,1536]{2,1,0:T(8,128)(2,1)} %param.22) | data formatting | bytes 9437184 | tf_op jit(solution)/shard_map/reshape;squeeze | solution.py:107
  34.1 10.3 %copy.231 = bf16[6,256,24,64]{1,3,2,0:T(8,128)(2,1)} copy(bf16[6,256,24,64]{3,2,1,0:T(8,128)(2,1)} %reshape.634) | data formatting | bytes 9437184
  46.2 8.0 %fusion.94 = f32[6,24,64,128]{3,2,1,0:T(8,128)} fusion(bf16[6,256,24,64]{1,3,2,0:T(8,128)(2,1)} %copy.231, f32[6,256,128]{1,2,0:T(8,128)S(1)} %copy.228, f32[6,24,256]{2,1,0:T(8,128)S(1)} %select_multiply_fusion.3), kind=kOutput, calls=%fused_computation.172 | convolution fusion | flops 613416960 | bytes 10371072 | tf_op jit(solution)/shard_map/jvp(cjhp,chjn->chpn)/dot_general | solution.py:31
  54.2 8.2 %while.108 = (s32[]{:T(128)}, f32[24,64,128]{2,1,0:T(8,128)S(1)}, f32[6,24]{1,0:T(8,128)S(1)}, f32[6,24,64,128]{3,2,1,0:T(8,128)}, s32[]{:T(128)}, /*index=5*/s32[]{:T(128)}) while((s32[]{:T(128)}, f32[24,64,128]{2,1,0:T(8,128)S(1)}, f32[6,24]{1,0:T(8,128)S(1)}, f32[6,24,64,128]{3,2,1,0:T(8,128)}, s32[]{:T(128)}, ...), condition=%wide.region_7.8_spmd.clone, body=%wide.region_6.7_spmd.clone.sunk | while | flops 589827 | bytes 2359671 | solution.py:42
  62.4 83.2 %all-gather.3.cloned.1.call-done = f32[64,12,64,128]{3,2,1,0:T(8,128)} async-done(((f32[1,12,64,128]{3,2,1,0:T(8,128)}), f32[64,12,64,128]{3,2,1,0:T(8,128)}) %all-gather.3.cloned.1.call-update) | async-done | bytes 25165840 | tf_op jit(solution)/shard_map/all_gather | solution.py:104
  146.6 2.7 all-gather
  154.8 2.8 broadcast.268.clone
  157.7 17.0 %while.105 = (s32[]{:T(128)}, f32[24,64,128]{2,1,0:T(8,128)S(1)}, f32[6,24,64,128]{3,2,1,0:T(8,128)}, f32[6,24,1,1]{1,3,2,0:T(1,128)}, f32[6,24]{1,0:T(8,128)S(1)}, /*index=5*/f32[6,24,64,128]{3,2,1,0:T(8,128)}, s32[]{:T(128)}) while((s32[]{:T(128)}, f32[24,64,128]{2,1,0:T(8,128)S(1)}, f32[6,24,64,128]{3,2,1,0:T(8,128)}, ...), condition=%wide.region_9.10_spmd, body=%wide.region_8.9_spmd.sunk | while | flops 393218 | bytes 3934165 | solution.py:42
  174.6 2.7 broadcast.268
  177.4 2.8 broadcast_in_dim.260
  181.7 195.7 %while.109 = (s32[]{:T(128)}, f32[24]{0:T(128)}, f32[24]{0:T(128)}, f32[24]{0:T(128)}, bf16[6,256,24,64]{1,3,2,0:T(8,128)(2,1)}, /*index=5*/bf16[6,256,256]{1,2,...) while((s32[]{:T(128)}, f32[24]{0:T(128)}, f32[24]{0:T(128)}, ...), condition=%wide.region_31.32_spmd.clone, body=%wide.region_16.31_spmd.clone.sunk | while | flops 2306163200 | bytes 22004424 | solution.py:79
  193.2 6.2 %fusion.183 = (f32[24,256]{1,0:T(8,128)S(1)}, f32[24,256]{1,0:T(8,128)S(1)}, f32[24,256]{1,0:T(8,128)}, bf16[256,256]{1,0:T(8,128)(2,1)S(1)}) fusion(f32[24,256]{1,0:T(8,128)S(1)} %copy_bitcast_fusion.13, f32[24,256]{1,0:T(8,128)} %get-tuple-element.1559, f32[256,256]{1,0:T(8,128)S(1)} %fusion.181, pred[256,256]{1,0:T(8,128)(4,1)S(1)} %fusion.182, ...), kind=kOutput, calls=%fused_computation.73.clone.1 | convolution fusion | flops 224835584 | bytes 2154496 | tf_op jit(solution)/shard_map/transpose(jvp())/while/body/eval_jaxpr/checkpoint/hij,jhp->ihp/dot_general | solution.py:55
  199.5 1.8 fusion.191
  201.5 2.6 fusion.190
  205.2 3.9 fusion.189
  209.5 2.5 reduce-window.160
  225.8 6.2 %fusion.183 = (f32[24,256]{1,0:T(8,128)S(1)}, f32[24,256]{1,0:T(8,128)S(1)}, f32[24,256]{1,0:T(8,128)}, bf16[256,256]{1,0:T(8,128)(2,1)S(1)}) fusion(f32[24,256]{1,0:T(8,128)S(1)} %copy_bitcast_fusion.13, f32[24,256]{1,0:T(8,128)} %get-tuple-element.1559, f32[256,256]{1,0:T(8,128)S(1)} %fusion.181, pred[256,256]{1,0:T(8,128)(4,1)S(1)} %fusion.182, ...), kind=kOutput, calls=%fused_computation.73.clone.1 | convolution fusion | flops 224835584 | bytes 2154496 | tf_op jit(solution)/shard_map/transpose(jvp())/while/body/eval_jaxpr/checkpoint/hij,jhp->ihp/dot_general | solution.py:55
  232.1 1.8 fusion.191
  234.1 2.6 fusion.190
  237.8 3.9 fusion.189
  242.1 2.5 reduce-window.160
  258.4 6.2 %fusion.183 = (f32[24,256]{1,0:T(8,128)S(1)}, f32[24,256]{1,0:T(8,128)S(1)}, f32[24,256]{1,0:T(8,128)}, bf16[256,256]{1,0:T(8,128)(2,1)S(1)}) fusion(f32[24,256]{1,0:T(8,128)S(1)} %copy_bitcast_fusion.13, f32[24,256]{1,0:T(8,128)} %get-tuple-element.1559, f32[256,256]{1,0:T(8,128)S(1)} %fusion.181, pred[256,256]{1,0:T(8,128)(4,1)S(1)} %fusion.182, ...), kind=kOutput, calls=%fused_computation.73.clone.1 | convolution fusion | flops 224835584 | bytes 2154496 | tf_op jit(solution)/shard_map/transpose(jvp())/while/body/eval_jaxpr/checkpoint/hij,jhp->ihp/dot_general | solution.py:55
  264.7 1.8 fusion.191
  266.7 2.6 fusion.190
  270.4 3.9 fusion.189
  274.7 2.5 reduce-window.160
  291.0 6.2 %fusion.183 = (f32[24,256]{1,0:T(8,128)S(1)}, f32[24,256]{1,0:T(8,128)S(1)}, f32[24,256]{1,0:T(8,128)}, bf16[256,256]{1,0:T(8,128)(2,1)S(1)}) fusion(f32[24,256]{1,0:T(8,128)S(1)} %copy_bitcast_fusion.13, f32[24,256]{1,0:T(8,128)} %get-tuple-element.1559, f32[256,256]{1,0:T(8,128)S(1)} %fusion.181, pred[256,256]{1,0:T(8,128)(4,1)S(1)} %fusion.182, ...), kind=kOutput, calls=%fused_computation.73.clone.1 | convolution fusion | flops 224835584 | bytes 2154496 | tf_op jit(solution)/shard_map/transpose(jvp())/while/body/eval_jaxpr/checkpoint/hij,jhp->ihp/dot_general | solution.py:55
  297.3 1.8 fusion.191
  299.3 2.6 fusion.190
  303.0 3.9 fusion.189
  307.3 2.5 reduce-window.160
  323.7 6.2 %fusion.183 = (f32[24,256]{1,0:T(8,128)S(1)}, f32[24,256]{1,0:T(8,128)S(1)}, f32[24,256]{1,0:T(8,128)}, bf16[256,256]{1,0:T(8,128)(2,1)S(1)}) fusion(f32[24,256]{1,0:T(8,128)S(1)} %copy_bitcast_fusion.13, f32[24,256]{1,0:T(8,128)} %get-tuple-element.1559, f32[256,256]{1,0:T(8,128)S(1)} %fusion.181, pred[256,256]{1,0:T(8,128)(4,1)S(1)} %fusion.182, ...), kind=kOutput, calls=%fused_computation.73.clone.1 | convolution fusion | flops 224835584 | bytes 2154496 | tf_op jit(solution)/shard_map/transpose(jvp())/while/body/eval_jaxpr/checkpoint/hij,jhp->ihp/dot_general | solution.py:55
  330.0 1.8 fusion.191
  332.0 2.6 fusion.190
  335.7 3.9 fusion.189
  340.0 2.5 reduce-window.160
  356.3 6.2 %fusion.183 = (f32[24,256]{1,0:T(8,128)S(1)}, f32[24,256]{1,0:T(8,128)S(1)}, f32[24,256]{1,0:T(8,128)}, bf16[256,256]{1,0:T(8,128)(2,1)S(1)}) fusion(f32[24,256]{1,0:T(8,128)S(1)} %copy_bitcast_fusion.13, f32[24,256]{1,0:T(8,128)} %get-tuple-element.1559, f32[256,256]{1,0:T(8,128)S(1)} %fusion.181, pred[256,256]{1,0:T(8,128)(4,1)S(1)} %fusion.182, ...), kind=kOutput, calls=%fused_computation.73.clone.1 | convolution fusion | flops 224835584 | bytes 2154496 | tf_op jit(solution)/shard_map/transpose(jvp())/while/body/eval_jaxpr/checkpoint/hij,jhp->ihp/dot_general | solution.py:55
  364.6 2.6 fusion.190
  368.3 3.9 fusion.189
  372.6 2.5 reduce-window.160
  377.5 11.6 %while.110 = (s32[]{:T(128)}, f32[24,64,128]{2,1,0:T(8,128)S(1)}, f32[6,24,64,128]{3,2,1,0:T(8,128)}, f32[6,24,1,1]{1,3,2,0:T(1,128)}, s32[]{:T(128)}, /*index=5*/s32[]{:T(128)}, s32[]{:T(128)}) while((s32[]{:T(128)}, f32[24,64,128]{2,1,0:T(8,128)S(1)}, f32[6,24,64,128]{3,2,1,0:T(8,128)}, f32[6,24,1,1]{1,3,2,0:T(1,128)}, ...), condition=%wide.region_33.34_spmd.clone, body=%wide.region_32.33_spmd.clone.sunk | while | flops 589828 | bytes 2359691 | solution.py:42
  390.1 2.3 collective-permute-start.1
  394.3 15.2 %while.106 = (s32[]{:T(128)}, f32[24,64,128]{2,1,0:T(8,128)S(1)}, bf16[6,24,64,128]{3,2,1,0:T(8,128)(2,1)S(1)}, f32[6,24]{1,0:T(8,128)S(1)}, f32[6,24,64,128]{3,...) while((s32[]{:T(128)}, f32[24,64,128]{2,1,0:T(8,128)S(1)}, ...), condition=%wide.region_36.37_spmd, body=%wide.region_34.36_spmd.sunk | while | flops 786411 | bytes 4719297 | solution.py:42
  410.9 7.1 %fusion.87 = (f32[6,24,256]{2,1,0:T(8,128)S(1)}, bf16[6,256,128]{1,2,0:T(8,128)(2,1)S(1)}) fusion(f32[6,256,128]{1,2,0:T(8,128)} %copy-done.6, f32[6,24,256]{2,1,0:T(8,128)S(1)} %copy-done.16, bf16[6,24,64,128]{3,2,1,0:T(8,128)(2,1)} %copy-done.4, bf16[6,256,24,64]{1,3,2,0:T(8,128)(2,1)} %get-tuple-element.1777), kind=kOutput, calls=%fused_computation.162 | convolution fusion | flops 627339264 | bytes 8552448 | tf_op jit(solution)/shard_map/transpose(jvp(cjhp,chjn->chpn))/dot_general | solution.py:31
  418.8 14.9 %reduce-window.130 = f32[6,24,2,128]{3,1,2,0:T(8,128)S(1)} reduce-window(f32[6,24,2,128]{3,1,2,0:T(8,128)S(1)} %copy_bitcast_fusion.5, f32[]{:T(128)} %constant.289.clone.1), window={size=1x1x1x128 pad=0_0x0_0x0_0x0_127}, to_apply=%region_40.41 | reduce-window | flops 4681728 | bytes 294916 | tf_op jit(solution)/shard_map/reduce-window.14
  436.3 6.9 %bitcast_add_fusion.6 = bf16[6,256,24,64]{1,3,2,0:T(8,128)(2,1)} fusion(bf16[6,256,24,64]{1,3,2,0:T(8,128)(2,1)} %get-tuple-element.766, bf16[6,24,64,128]{3,2,1,0:T(8,128)(2,1)} %copy-done.4, f32[6,256,128]{1,2,0:T(8,128)S(1)} %copy-done.7, f32[6,24,256]{2,1,0:T(8,128)S(1)} %copy-done.16), kind=kOutput, calls=%fused_computation.171 | convolution fusion | flops 615776256 | bytes 12730368 | tf_op jit(solution)/shard_map/transpose(jvp(cjhp,chjn->chpn))/dot_general | solution.py:31
  443.2 10.4 %copy.250 = bf16[6,256,24,64]{3,2,1,0:T(8,128)(2,1)} copy(bf16[6,256,24,64]{1,3,2,0:T(8,128)(2,1)} %bitcast_add_fusion.6) | data formatting | bytes 9437184
  453.6 13.1 %reshape.633 = bf16[1,1536,1536]{2,1,0:T(8,128)(2,1)} reshape(bf16[6,256,24,64]{3,2,1,0:T(8,128)(2,1)} %copy.250) | data formatting | bytes 9437184
  467.4 62.6 %while.107 = (s32[]{:T(128)}, bf16[6,256,1536]{2,1,0:T(8,128)(2,1)}, bf16[6,256,24,64]{1,3,2,0:T(8,128)(2,1)}, bf16[6,256,256]{2,1,0:T(8,128)(2,1)}, s32[6,256]{...) while((s32[]{:T(128)}, bf16[6,256,1536]{2,1,0:T(8,128)(2,1)}, ...), condition=%wide.region_15.16_spmd.clone, body=%wide.region_10.15_spmd.clone.sunk | while | flops 833433920 | bytes 10981461 | solution.py:79
  471.2 1.9 fusion.163
  473.3 3.5 fusion.167
  481.6 1.9 fusion.163
  483.7 3.4 fusion.167
  491.9 1.9 fusion.163
  494.0 3.6 fusion.167
  502.4 1.9 fusion.163
  504.5 3.4 fusion.167
  512.6 1.9 fusion.163
  514.8 3.6 fusion.167
  523.1 1.9 fusion.163
  525.2 3.5 fusion.167
  530.0 64.5 %all-reduce.5 = (f32[24]{0:T(128)}, f32[24]{0:T(128)}, f32[24]{0:T(128)}) all-reduce(f32[24]{0:T(128)S(1)} %get-tuple-element.1226, f32[24]{0:T(128)S(1)} %add.228, f32[24]{0:T(128)S(1)} %copy-done.26), channel_id=1, replica_groups=mesh['stream'=64,'seq'=2] {'stream','seq'}, use_global_device_ids=true, to_apply=%region_43.44 | all-reduce | flops 72 | bytes 576 | tf_op jit(solution)/shard_map/psum | solution.py:154
  (677 shorter events, 199.5 us)
Async XLA Ops:
  7.2 138.5 %all-gather.3.cloned.1.call-start = ((), (), s32[]{:S(2)}) async-start(), calls=%async_computation | async-start | bytes 25559040 | tf_op jit(solution)/shard_map/all_gather | solution.py:104
  14.3 19.8 %copy-start.32 = (f32[24]{0:T(128)}, f32[24]{0:T(128)S(1)}, u32[]{:S(2)}) copy-start(f32[24]{0:T(128)S(1)} %exp.90) | copy-start | bytes 292
  16.1 29.9 %copy-start.1 = (f32[6,24,256]{2,1,0:T(8,128)}, f32[6,24,256]{2,1,0:T(8,128)S(1)}, u32[]{:S(2)}) copy-start(f32[6,24,256]{2,1,0:T(8,128)S(1)} %get-tuple-element.1738) | copy-start | bytes 442372
  19.9 26.1 %copy-start.11 = (f32[6,24,2]{1,2,0:T(2,128)}, f32[6,24,2]{1,2,0:T(2,128)S(1)}, u32[]{:S(2)}) copy-start(f32[6,24,2]{1,2,0:T(2,128)S(1)} %slice.164) | copy-start | bytes 3460
  21.2 25.0 %copy-start.6 = (f32[6,256,128]{1,2,0:T(8,128)}, f32[6,256,128]{1,2,0:T(8,128)S(1)}, u32[]{:S(2)}) copy-start(f32[6,256,128]{1,2,0:T(8,128)S(1)} %copy.228) | copy-start | bytes 2359300
  34.1 11.9 %copy-start.10 = (f32[24]{0:T(128)S(1)}, f32[24]{0:T(128)}, u32[]{:S(2)}) copy-start(f32[24]{0:T(128)} %param.26) | copy-start | bytes 292
  45.3 8.9 %copy-start.13 = (f32[6,24]{1,0:T(8,128)}, f32[6,24]{1,0:T(8,128)S(1)}, u32[]{:S(2)}) copy-start(f32[6,24]{1,0:T(8,128)S(1)} %slice_reduce_fusion.7) | copy-start | bytes 1732
  46.0 8.2 %copy-start.19 = (pred[6,256]{1,0:T(8,128)(4,1)}, pred[6,256]{1,0:T(8,128)(4,1)S(1)}, u32[]{:S(2)}) copy-start(pred[6,256]{1,0:T(8,128)(4,1)S(1)} %broadcast_compare_fusion.2) | copy-start | bytes 4612
  46.2 8.0 %copy-start.15 = (f32[6,24,256]{2,1,0:T(8,128)}, f32[6,24,256]{2,1,0:T(8,128)S(1)}, u32[]{:S(2)}) copy-start(f32[6,24,256]{2,1,0:T(8,128)S(1)} %select_multiply_fusion.3) | copy-start | bytes 442372
  150.3 4.4 collective-permute-start
  193.0 6.4 %copy-start.5 = (pred[256,256]{1,0:T(8,128)(4,1)}, pred[256,256]{1,0:T(8,128)(4,1)S(1)}, u32[]{:S(2)}) copy-start(pred[256,256]{1,0:T(8,128)(4,1)S(1)} %fusion.182) | copy-start | bytes 196612 | tf_op jit(solution)/shard_map/transpose(jvp())/while
  193.2 6.2 %copy-start = (f32[256,256]{1,0:T(8,128)}, f32[256,256]{1,0:T(8,128)S(1)}, u32[]{:S(2)}) copy-start(f32[256,256]{1,0:T(8,128)S(1)} %fusion.181) | copy-start | bytes 786436 | tf_op jit(solution)/shard_map/transpose(jvp())/while
  205.1 7.0 %copy-start.8 = (f32[24,256]{1,0:T(8,128)S(1)}, f32[24,256]{1,0:T(8,128)}, u32[]{:S(2)}) copy-start(f32[24,256]{1,0:T(8,128)} %get-tuple-element.1568) | copy-start | bytes 73732 | tf_op jit(solution)/shard_map/transpose(jvp())/while
  205.1 7.0 %copy-start.18 = (f32[24]{0:T(128)S(1)}, f32[24]{0:T(128)}, u32[]{:S(2)}) copy-start(f32[24]{0:T(128)} %copy-done.17) | copy-start | bytes 292 | tf_op jit(solution)/shard_map/transpose(jvp())/while
  205.2 8.0 %copy-start.21 = (f32[24]{0:T(128)S(1)}, f32[24]{0:T(128)}, u32[]{:S(2)}) copy-start(f32[24]{0:T(128)} %get-tuple-element.1641) | copy-start | bytes 292 | tf_op jit(solution)/shard_map/transpose(jvp())/while
  205.2 8.0 %copy-start.27 = (f32[24]{0:T(128)S(1)}, f32[24]{0:T(128)}, u32[]{:S(2)}) copy-start(f32[24]{0:T(128)} %get-tuple-element.1642) | copy-start | bytes 292 | tf_op jit(solution)/shard_map/transpose(jvp())/while
  209.4 4.4 copy-start.25
  225.6 6.4 %copy-start.5 = (pred[256,256]{1,0:T(8,128)(4,1)}, pred[256,256]{1,0:T(8,128)(4,1)S(1)}, u32[]{:S(2)}) copy-start(pred[256,256]{1,0:T(8,128)(4,1)S(1)} %fusion.182) | copy-start | bytes 196612 | tf_op jit(solution)/shard_map/transpose(jvp())/while
  225.8 6.2 %copy-start = (f32[256,256]{1,0:T(8,128)}, f32[256,256]{1,0:T(8,128)S(1)}, u32[]{:S(2)}) copy-start(f32[256,256]{1,0:T(8,128)S(1)} %fusion.181) | copy-start | bytes 786436 | tf_op jit(solution)/shard_map/transpose(jvp())/while
  237.8 7.0 %copy-start.8 = (f32[24,256]{1,0:T(8,128)S(1)}, f32[24,256]{1,0:T(8,128)}, u32[]{:S(2)}) copy-start(f32[24,256]{1,0:T(8,128)} %get-tuple-element.1568) | copy-start | bytes 73732 | tf_op jit(solution)/shard_map/transpose(jvp())/while
  237.8 7.0 %copy-start.18 = (f32[24]{0:T(128)S(1)}, f32[24]{0:T(128)}, u32[]{:S(2)}) copy-start(f32[24]{0:T(128)} %copy-done.17) | copy-start | bytes 292 | tf_op jit(solution)/shard_map/transpose(jvp())/while
  237.8 8.0 %copy-start.21 = (f32[24]{0:T(128)S(1)}, f32[24]{0:T(128)}, u32[]{:S(2)}) copy-start(f32[24]{0:T(128)} %get-tuple-element.1641) | copy-start | bytes 292 | tf_op jit(solution)/shard_map/transpose(jvp())/while
  237.8 8.0 %copy-start.27 = (f32[24]{0:T(128)S(1)}, f32[24]{0:T(128)}, u32[]{:S(2)}) copy-start(f32[24]{0:T(128)} %get-tuple-element.1642) | copy-start | bytes 292 | tf_op jit(solution)/shard_map/transpose(jvp())/while
  242.1 4.4 copy-start.25
  258.2 6.4 %copy-start.5 = (pred[256,256]{1,0:T(8,128)(4,1)}, pred[256,256]{1,0:T(8,128)(4,1)S(1)}, u32[]{:S(2)}) copy-start(pred[256,256]{1,0:T(8,128)(4,1)S(1)} %fusion.182) | copy-start | bytes 196612 | tf_op jit(solution)/shard_map/transpose(jvp())/while
  258.4 6.2 %copy-start = (f32[256,256]{1,0:T(8,128)}, f32[256,256]{1,0:T(8,128)S(1)}, u32[]{:S(2)}) copy-start(f32[256,256]{1,0:T(8,128)S(1)} %fusion.181) | copy-start | bytes 786436 | tf_op jit(solution)/shard_map/transpose(jvp())/while
  270.4 7.0 %copy-start.8 = (f32[24,256]{1,0:T(8,128)S(1)}, f32[24,256]{1,0:T(8,128)}, u32[]{:S(2)}) copy-start(f32[24,256]{1,0:T(8,128)} %get-tuple-element.1568) | copy-start | bytes 73732 | tf_op jit(solution)/shard_map/transpose(jvp())/while
  270.4 7.0 %copy-start.18 = (f32[24]{0:T(128)S(1)}, f32[24]{0:T(128)}, u32[]{:S(2)}) copy-start(f32[24]{0:T(128)} %copy-done.17) | copy-start | bytes 292 | tf_op jit(solution)/shard_map/transpose(jvp())/while
  270.4 8.0 %copy-start.21 = (f32[24]{0:T(128)S(1)}, f32[24]{0:T(128)}, u32[]{:S(2)}) copy-start(f32[24]{0:T(128)} %get-tuple-element.1641) | copy-start | bytes 292 | tf_op jit(solution)/shard_map/transpose(jvp())/while
  270.4 8.0 %copy-start.27 = (f32[24]{0:T(128)S(1)}, f32[24]{0:T(128)}, u32[]{:S(2)}) copy-start(f32[24]{0:T(128)} %get-tuple-element.1642) | copy-start | bytes 292 | tf_op jit(solution)/shard_map/transpose(jvp())/while
  290.8 6.4 %copy-start.5 = (pred[256,256]{1,0:T(8,128)(4,1)}, pred[256,256]{1,0:T(8,128)(4,1)S(1)}, u32[]{:S(2)}) copy-start(pred[256,256]{1,0:T(8,128)(4,1)S(1)} %fusion.182) | copy-start | bytes 196612 | tf_op jit(solution)/shard_map/transpose(jvp())/while
  291.0 6.2 %copy-start = (f32[256,256]{1,0:T(8,128)}, f32[256,256]{1,0:T(8,128)S(1)}, u32[]{:S(2)}) copy-start(f32[256,256]{1,0:T(8,128)S(1)} %fusion.181) | copy-start | bytes 786436 | tf_op jit(solution)/shard_map/transpose(jvp())/while
  303.0 7.0 %copy-start.8 = (f32[24,256]{1,0:T(8,128)S(1)}, f32[24,256]{1,0:T(8,128)}, u32[]{:S(2)}) copy-start(f32[24,256]{1,0:T(8,128)} %get-tuple-element.1568) | copy-start | bytes 73732 | tf_op jit(solution)/shard_map/transpose(jvp())/while
  303.0 7.0 %copy-start.18 = (f32[24]{0:T(128)S(1)}, f32[24]{0:T(128)}, u32[]{:S(2)}) copy-start(f32[24]{0:T(128)} %copy-done.17) | copy-start | bytes 292 | tf_op jit(solution)/shard_map/transpose(jvp())/while
  303.0 8.0 %copy-start.21 = (f32[24]{0:T(128)S(1)}, f32[24]{0:T(128)}, u32[]{:S(2)}) copy-start(f32[24]{0:T(128)} %get-tuple-element.1641) | copy-start | bytes 292 | tf_op jit(solution)/shard_map/transpose(jvp())/while
  303.0 8.0 %copy-start.27 = (f32[24]{0:T(128)S(1)}, f32[24]{0:T(128)}, u32[]{:S(2)}) copy-start(f32[24]{0:T(128)} %get-tuple-element.1642) | copy-start | bytes 292 | tf_op jit(solution)/shard_map/transpose(jvp())/while
  323.5 6.4 %copy-start.5 = (pred[256,256]{1,0:T(8,128)(4,1)}, pred[256,256]{1,0:T(8,128)(4,1)S(1)}, u32[]{:S(2)}) copy-start(pred[256,256]{1,0:T(8,128)(4,1)S(1)} %fusion.182) | copy-start | bytes 196612 | tf_op jit(solution)/shard_map/transpose(jvp())/while
  323.7 6.2 %copy-start = (f32[256,256]{1,0:T(8,128)}, f32[256,256]{1,0:T(8,128)S(1)}, u32[]{:S(2)}) copy-start(f32[256,256]{1,0:T(8,128)S(1)} %fusion.181) | copy-start | bytes 786436 | tf_op jit(solution)/shard_map/transpose(jvp())/while
  335.7 7.0 %copy-start.8 = (f32[24,256]{1,0:T(8,128)S(1)}, f32[24,256]{1,0:T(8,128)}, u32[]{:S(2)}) copy-start(f32[24,256]{1,0:T(8,128)} %get-tuple-element.1568) | copy-start | bytes 73732 | tf_op jit(solution)/shard_map/transpose(jvp())/while
  335.7 7.0 %copy-start.18 = (f32[24]{0:T(128)S(1)}, f32[24]{0:T(128)}, u32[]{:S(2)}) copy-start(f32[24]{0:T(128)} %copy-done.17) | copy-start | bytes 292 | tf_op jit(solution)/shard_map/transpose(jvp())/while
  335.7 8.0 %copy-start.21 = (f32[24]{0:T(128)S(1)}, f32[24]{0:T(128)}, u32[]{:S(2)}) copy-start(f32[24]{0:T(128)} %get-tuple-element.1641) | copy-start | bytes 292 | tf_op jit(solution)/shard_map/transpose(jvp())/while
  335.7 8.0 %copy-start.27 = (f32[24]{0:T(128)S(1)}, f32[24]{0:T(128)}, u32[]{:S(2)}) copy-start(f32[24]{0:T(128)} %get-tuple-element.1642) | copy-start | bytes 292 | tf_op jit(solution)/shard_map/transpose(jvp())/while
  356.1 6.4 %copy-start.5 = (pred[256,256]{1,0:T(8,128)(4,1)}, pred[256,256]{1,0:T(8,128)(4,1)S(1)}, u32[]{:S(2)}) copy-start(pred[256,256]{1,0:T(8,128)(4,1)S(1)} %fusion.182) | copy-start | bytes 196612 | tf_op jit(solution)/shard_map/transpose(jvp())/while
  356.3 6.2 %copy-start = (f32[256,256]{1,0:T(8,128)}, f32[256,256]{1,0:T(8,128)S(1)}, u32[]{:S(2)}) copy-start(f32[256,256]{1,0:T(8,128)S(1)} %fusion.181) | copy-start | bytes 786436 | tf_op jit(solution)/shard_map/transpose(jvp())/while
  368.3 7.0 %copy-start.8 = (f32[24,256]{1,0:T(8,128)S(1)}, f32[24,256]{1,0:T(8,128)}, u32[]{:S(2)}) copy-start(f32[24,256]{1,0:T(8,128)} %get-tuple-element.1568) | copy-start | bytes 73732 | tf_op jit(solution)/shard_map/transpose(jvp())/while
  368.3 7.0 %copy-start.18 = (f32[24]{0:T(128)S(1)}, f32[24]{0:T(128)}, u32[]{:S(2)}) copy-start(f32[24]{0:T(128)} %copy-done.17) | copy-start | bytes 292 | tf_op jit(solution)/shard_map/transpose(jvp())/while
  368.3 8.0 %copy-start.21 = (f32[24]{0:T(128)S(1)}, f32[24]{0:T(128)}, u32[]{:S(2)}) copy-start(f32[24]{0:T(128)} %get-tuple-element.1641) | copy-start | bytes 292 | tf_op jit(solution)/shard_map/transpose(jvp())/while
  368.3 8.0 %copy-start.27 = (f32[24]{0:T(128)S(1)}, f32[24]{0:T(128)}, u32[]{:S(2)}) copy-start(f32[24]{0:T(128)} %get-tuple-element.1642) | copy-start | bytes 292 | tf_op jit(solution)/shard_map/transpose(jvp())/while
  377.5 11.6 %copy-start.34 = (f32[24]{0:T(128)S(1)}, f32[24]{0:T(128)}, u32[]{:S(2)}) copy-start(f32[24]{0:T(128)} %broadcast_multiply_fusion) | copy-start | bytes 292
  390.1 4.1 collective-permute-start.1
  394.2 15.2 %copy-start.14 = (f32[6,24]{1,0:T(8,128)S(1)}, f32[6,24]{1,0:T(8,128)}, u32[]{:S(2)}) copy-start(f32[6,24]{1,0:T(8,128)} %copy-done.13) | copy-start | bytes 1732
  394.2 15.2 %copy-start.31 = (pred[6]{0:T(512)(128)(4,1)S(1)}, pred[6]{0:T(512)(128)(4,1)}, u32[]{:S(2)}) copy-start(pred[6]{0:T(512)(128)(4,1)} %copy-done.30) | copy-start | bytes 22
  394.2 16.6 %copy-start.16 = (f32[6,24,256]{2,1,0:T(8,128)S(1)}, f32[6,24,256]{2,1,0:T(8,128)}, u32[]{:S(2)}) copy-start(f32[6,24,256]{2,1,0:T(8,128)} %copy-done.15) | copy-start | bytes 442372
  410.9 7.1 %copy-start.2 = (f32[6,24,256]{2,1,0:T(8,128)S(1)}, f32[6,24,256]{2,1,0:T(8,128)}, u32[]{:S(2)}) copy-start(f32[6,24,256]{2,1,0:T(8,128)} %get-tuple-element.1779) | copy-start | bytes 442372
  410.9 7.1 %copy-start.12 = (f32[6,24,2]{1,2,0:T(2,128)S(1)}, f32[6,24,2]{1,2,0:T(2,128)}, u32[]{:S(2)}) copy-start(f32[6,24,2]{1,2,0:T(2,128)} %copy-done.11) | copy-start | bytes 3460
  410.9 7.1 %copy-start.20 = (pred[6,256]{1,0:T(8,128)(4,1)S(1)}, pred[6,256]{1,0:T(8,128)(4,1)}, u32[]{:S(2)}) copy-start(pred[6,256]{1,0:T(8,128)(4,1)} %copy-done.19) | copy-start | bytes 4612
  410.9 23.0 %copy-start.33 = (f32[24]{0:T(128)S(1)}, f32[24]{0:T(128)}, u32[]{:S(2)}) copy-start(f32[24]{0:T(128)} %copy-done.32) | copy-start | bytes 292
  410.9 23.4 %copy-start.9 = (f32[6,24,256]{2,1,0:T(8,128)S(1)}, f32[6,24,256]{2,1,0:T(8,128)}, u32[]{:S(2)}) copy-start(f32[6,24,256]{2,1,0:T(8,128)} %get-tuple-element.772) | copy-start | bytes 442372
  410.9 24.2 %copy-start.3 = (bf16[6,256,256]{1,2,0:T(8,128)(2,1)S(1)}, bf16[6,256,256]{1,2,0:T(8,128)(2,1)}, u32[]{:S(2)}) copy-start(bf16[6,256,256]{1,2,0:T(8,128)(2,1)} %get-tuple-element.771) | copy-start | bytes 2359300
  418.0 18.4 %copy-start.7 = (f32[6,256,128]{1,2,0:T(8,128)S(1)}, f32[6,256,128]{1,2,0:T(8,128)}, u32[]{:S(2)}) copy-start(f32[6,256,128]{1,2,0:T(8,128)} %copy-done.6) | copy-start | bytes 2359300
  453.6 13.1 %copy-start.23 = (f32[24]{0:T(128)S(1)}, f32[24]{0:T(128)}, u32[]{:S(2)}) copy-start(f32[24]{0:T(128)} %get-tuple-element.774) | copy-start | bytes 292
  453.6 13.7 %copy-start.35 = (f32[24]{0:T(128)S(1)}, f32[24]{0:T(128)}, u32[]{:S(2)}) copy-start(f32[24]{0:T(128)} %get-tuple-element.1787) | copy-start | bytes 292
  467.4 62.7 %copy-start.29 = (f32[24]{0:T(128)S(1)}, f32[24]{0:T(128)}, u32[]{:S(2)}) copy-start(f32[24]{0:T(128)} %get-tuple-element.775) | copy-start | bytes 292
  467.4 62.7 %copy-start.26 = (f32[24]{0:T(128)S(1)}, f32[24]{0:T(128)}, u32[]{:S(2)}) copy-start(f32[24]{0:T(128)} %get-tuple-element.776) | copy-start | bytes 292
  (30 other events, 55.7 us)
Sparse Core Ops, SparseCore 0:
  10.8 134.8 all-gather.2
where the time goes:
time: 607 us; the launch traced here: 601 us
  local copies, waits for them, and re-layouts  158 us (26%)
  matrix products  151 us (25%)
  other arithmetic  115 us (19%)
  waiting for transfers between devices  86.9 us (14%)
  blocking collectives  67.2 us (11%)
  between operations  16.4 us (3%)
    all_gather x1, waiting for transfers between devices, shards(): gathered = lax.all_gather(old_states, 'stream', axis=0, tiled=True)  83.2 us
    dot_general x18, matrix products, one_group(): jnp.einsum('hij,jhp->ihp', mixing, inputs_q, preferred_element_type=jnp.f...  81.8 us
    psum x1, blocking collectives, shards(): lax.psum((rates_first + rates_second, bias_first + bias_second, skip_tota...  64.5 us
    another operation x80, other arithmetic  52.5 us
    dot_general x24, matrix products, one_group(): jnp.einsum('in,hpn->ihp', c_part.astype(jnp.float32), starts_q, precision...  43.1 us
    unnamed x56, local copies, waits for them, and re-layouts  35.7 us
    squeeze x30, local copies, waits for them, and re-layouts, outputs(): lax.scan(per_group, 0, (inputs_c, maps_c, logits_c, flags_c, starts_c))  22.8 us
    dot_general x3, matrix products, group_states(): jnp.einsum('cjhp,chjn->chpn', inputs_c, b_weighted, preferred_element_typ...  21.9 us
  transfers between devices with their start and end apart: 3, of which 3 were waited for; matrix products, arithmetic and copies ran while one was open for 9% of the time, Pallas kernels for 0%

commit v1 on v0

--- a/solution.py
+++ b/solution.py
@@ -101,7 +101,9 @@
     stream_index = lax.axis_index("stream")
     position = seq_index * length + lax.iota(jnp.int32, length)
     reset_flags = jnp.any(doc_starts[0][:, None] == position[None, :], axis=0).astype(jnp.int32)
-    gathered = lax.all_gather(old_states, "stream", axis=0, tiled=True)
+    gathered = jnp.concatenate(
+        lax.all_to_all(jnp.stack([old_states] * lax.axis_size("stream")), "stream", 0, 0), axis=0
+    )
     own_block = lax.dynamic_index_in_dim(gathered, old_owner[stream_index], 0, keepdims=False)
     start_state = lax.all_gather(own_block, "seq", axis=0, tiled=True)
     inputs_c = head_inputs[0].reshape(groups, GROUP, head_count, head_dim)

time: 607 us -> 935 us (1.54)
  waiting for transfers between devices: 86.9 us -> 398 us
  between operations: 16.4 us -> 3.1 us
  starting transfers between devices: 3.8 us -> 16.1 us
  local copies, waits for them, and re-layouts: 158 us -> 169 us
    all_to_all x0 -> x1, waiting for transfers between devices: none -> 395 us  [shards(): lax.all_to_all(jnp.stack([old_states] * lax.axis_size('stream')), 'stream...]
    all_gather x1 -> x0, waiting for transfers between devices: 83.2 us -> none  [shards(): gathered = lax.all_gather(old_states, 'stream', axis=0, tiled=True)]
    another operation x83 -> x84, local copies, waits for them, and re-layouts: 11 us -> 23.6 us  [the longest x1 12.5 us: shards(): jnp.stack([old_states] * lax.axis_size('stream'))]
    all_to_all x0 -> x1, starting transfers between devices: none -> 12.3 us  [shards(): lax.all_to_all(jnp.stack([old_states] * lax.axis_size('stream')), 'stream...]
    unnamed x56 -> x64, local copies, waits for them, and re-layouts: 35.7 us -> 35.6 us
  transfers between devices with their start and end apart: 3 -> 3, of which waited for: 3 -> 3; matrix products, arithmetic and copies ran while one was open for 9% -> 5% of each run, Pallas kernels for 0% -> 0%
where the time goes in v1:
time: 935 us; the launch traced here: 929 us
  waiting for transfers between devices  398 us (43%)
  local copies, waits for them, and re-layouts  169 us (18%)
  matrix products  151 us (16%)
  other arithmetic  113 us (12%)
  blocking collectives  76.2 us (8%)
  starting transfers between devices  16.1 us (2%)
    all_to_all x1, waiting for transfers between devices, shards(): lax.all_to_all(jnp.stack([old_states] * lax.axis_size('stream')), 'stream...  395 us
    dot_general x18, matrix products, one_group(): jnp.einsum('hij,jhp->ihp', mixing, inputs_q, preferred_element_type=jnp.f...  81.8 us
    psum x1, blocking collectives, shards(): lax.psum((rates_first + rates_second, bias_first + bias_second, skip_tota...  72.1 us
    another operation x80, other arithmetic  52.5 us
    dot_general x24, matrix products, one_group(): jnp.einsum('in,hpn->ihp', c_part.astype(jnp.float32), starts_q, precision...  43.1 us
    unnamed x64, local copies, waits for them, and re-layouts  35.6 us
    squeeze x30, local copies, waits for them, and re-layouts, outputs(): lax.scan(per_group, 0, (inputs_c, maps_c, logits_c, flags_c, starts_c))  22.8 us
    dot_general x3, matrix products, group_states(): jnp.einsum('cjhp,chjn->chpn', inputs_c, b_weighted, preferred_element_typ...  21.9 us
  transfers between devices with their start and end apart: 3, of which 3 were waited for; matrix products, arithmetic and copies ran while one was open for 5% of the time, Pallas kernels for 0%

profile of v1, /device:TPU:1, one launch (start us, length us, event | category | flops | bytes accessed | tf_op | source)
XLA Modules:
  0.0 929.1 jit_solution(4669470102375340444)
XLA Ops:
  0.6 12.5 %stack.2 = f32[64,1,12,64,128]{4,3,1,2,0:T(8,128)} broadcast(f32[12,64,128]{2,1,0:T(8,128)} %bitcast.404), dimensions={2,3,4} | broadcast | bytes 25559040 | tf_op jit(solution)/shard_map/stack | solution.py:105
  13.2 12.3 %all-to-all-start = ((f32[64,1,12,64,128]{4,3,1,2,0:T(8,128)}), f32[64,1,12,64,128]{4,3,1,2,0:T(8,128)}, u32[]{:S(2)}, u32[]{:S(2)}) async-start(f32[64,1,12,64,128]{4,3,1,2,0:T(8,128)} %stack.2), calls=%async_computation | async-start | bytes 50331648 | tf_op jit(solution)/shard_map/all_to_all | solution.py:105
  27.6 1.8 reduce-window.126
  30.9 3.5 reduce-window.128
  35.0 12.8 %reshape.640 = bf16[6,256,24,64]{3,2,1,0:T(8,128)(2,1)} reshape(bf16[1,1536,1536]{2,1,0:T(8,128)(2,1)} %param.22) | data formatting | bytes 9437184 | tf_op jit(solution)/shard_map/reshape;squeeze | solution.py:109
  47.8 10.3 %copy.263 = bf16[6,256,24,64]{1,3,2,0:T(8,128)(2,1)} copy(bf16[6,256,24,64]{3,2,1,0:T(8,128)(2,1)} %reshape.640) | data formatting | bytes 9437184
  59.9 8.0 fusion.94
  67.8 7.9 while.108
  75.7 395.5 %all-to-all-done = f32[64,1,12,64,128]{4,3,1,2,0:T(8,128)} async-done(((f32[64,1,12,64,128]{4,3,1,2,0:T(8,128)}), f32[64,1,12,64,128]{4,3,1,2,0:T(8,128)}, u32[]{:S(2)}, u32[]{:S(2)}) %all-to-all-start) | async-done | bytes 25165856 | tf_op jit(solution)/shard_map/all_to_all | solution.py:105
  472.2 4.1 all-gather
  481.8 2.8 broadcast.271.clone
  484.6 17.0 %while.105 = (s32[]{:T(128)}, f32[24,64,128]{2,1,0:T(8,128)S(1)}, f32[6,24,64,128]{3,2,1,0:T(8,128)}, f32[6,24,1,1]{1,3,2,0:T(1,128)}, f32[6,24]{1,0:T(8,128)S(1)}, /*index=5*/f32[6,24,64,128]{3,2,1,0:T(8,128)}, s32[]{:T(128)}) while((s32[]{:T(128)}, f32[24,64,128]{2,1,0:T(8,128)S(1)}, f32[6,24,64,128]{3,2,1,0:T(8,128)}, ...), condition=%wide.region_9.10_spmd, body=%wide.region_8.9_spmd.sunk | while | flops 393218 | bytes 3934165 | solution.py:42
  501.6 2.7 broadcast.271
  504.3 2.8 broadcast_in_dim.260
  508.7 195.7 %while.109 = (s32[]{:T(128)}, f32[24]{0:T(128)}, f32[24]{0:T(128)}, f32[24]{0:T(128)}, bf16[6,256,24,64]{1,3,2,0:T(8,128)(2,1)}, /*index=5*/bf16[6,256,256]{1,2,...) while((s32[]{:T(128)}, f32[24]{0:T(128)}, f32[24]{0:T(128)}, ...), condition=%wide.region_31.32_spmd.clone, body=%wide.region_16.31_spmd.clone.sunk | while | flops 2306163200 | bytes 22004424 | solution.py:79
  520.2 6.2 fusion.183
  528.4 2.6 fusion.190
  532.1 3.9 fusion.189
  536.4 2.5 reduce-window.160
  552.8 6.2 fusion.183
  561.1 2.6 fusion.190
  564.8 3.9 fusion.189
  569.1 2.5 reduce-window.160
  585.4 6.2 fusion.183
  591.7 1.8 fusion.191
  593.7 2.6 fusion.190
  597.4 3.9 fusion.189
  601.7 2.5 reduce-window.160
  618.0 6.2 fusion.183
  624.3 1.8 fusion.191
  626.3 2.6 fusion.190
  630.0 3.9 fusion.189
  634.3 2.5 reduce-window.160
  650.6 6.2 fusion.183
  656.9 1.8 fusion.191
  659.0 2.6 fusion.190
  662.7 3.9 fusion.189
  666.9 2.5 reduce-window.160
  683.3 6.2 fusion.183
  691.6 2.6 fusion.190
  695.3 3.9 fusion.189
  699.6 2.5 reduce-window.160
  704.5 11.6 %while.110 = (s32[]{:T(128)}, f32[24,64,128]{2,1,0:T(8,128)S(1)}, f32[6,24,64,128]{3,2,1,0:T(8,128)}, f32[6,24,1,1]{1,3,2,0:T(1,128)}, s32[]{:T(128)}, /*index=5*/s32[]{:T(128)}, s32[]{:T(128)}) while((s32[]{:T(128)}, f32[24,64,128]{2,1,0:T(8,128)S(1)}, f32[6,24,64,128]{3,2,1,0:T(8,128)}, f32[6,24,1,1]{1,3,2,0:T(1,128)}, ...), condition=%wide.region_33.34_spmd.clone, body=%wide.region_32.33_spmd.clone.sunk | while | flops 589828 | bytes 2359691 | solution.py:42
  717.1 2.3 collective-permute-start.1
  721.2 15.2 %while.106 = (s32[]{:T(128)}, f32[24,64,128]{2,1,0:T(8,128)S(1)}, bf16[6,24,64,128]{3,2,1,0:T(8,128)(2,1)S(1)}, f32[6,24]{1,0:T(8,128)S(1)}, f32[6,24,64,128]{3,...) while((s32[]{:T(128)}, f32[24,64,128]{2,1,0:T(8,128)S(1)}, ...), condition=%wide.region_36.37_spmd, body=%wide.region_34.36_spmd.sunk | while | flops 786411 | bytes 4719297 | solution.py:42
  737.9 7.1 fusion.87
  745.7 14.9 %reduce-window.130 = f32[6,24,2,128]{3,1,2,0:T(8,128)S(1)} reduce-window(f32[6,24,2,128]{3,1,2,0:T(8,128)S(1)} %copy_bitcast_fusion.5, f32[]{:T(128)} %constant.290.clone.1), window={size=1x1x1x128 pad=0_0x0_0x0_0x0_127}, to_apply=%region_40.41 | reduce-window | flops 4681728 | bytes 294916 | tf_op jit(solution)/shard_map/reduce-window.14
  763.3 6.9 bitcast_add_fusion.6
  770.2 10.4 %copy.282 = bf16[6,256,24,64]{3,2,1,0:T(8,128)(2,1)} copy(bf16[6,256,24,64]{1,3,2,0:T(8,128)(2,1)} %bitcast_add_fusion.6) | data formatting | bytes 9437184
  780.6 13.1 %reshape.639 = bf16[1,1536,1536]{2,1,0:T(8,128)(2,1)} reshape(bf16[6,256,24,64]{3,2,1,0:T(8,128)(2,1)} %copy.282) | data formatting | bytes 9437184
  794.3 62.6 %while.107 = (s32[]{:T(128)}, bf16[6,256,1536]{2,1,0:T(8,128)(2,1)}, bf16[6,256,24,64]{1,3,2,0:T(8,128)(2,1)}, bf16[6,256,256]{2,1,0:T(8,128)(2,1)}, s32[6,256]{...) while((s32[]{:T(128)}, bf16[6,256,1536]{2,1,0:T(8,128)(2,1)}, ...), condition=%wide.region_15.16_spmd.clone, body=%wide.region_10.15_spmd.clone.sunk | while | flops 833433920 | bytes 10981461 | solution.py:79
  798.2 1.9 fusion.163
  800.3 3.5 fusion.167
  808.5 1.9 fusion.163
  810.6 3.5 fusion.167
  818.9 1.9 fusion.163
  821.0 3.5 fusion.167
  829.3 1.9 fusion.163
  831.4 3.5 fusion.167
  839.7 1.9 fusion.163
  841.8 3.4 fusion.167
  850.0 1.9 fusion.163
  852.1 3.6 fusion.167
  856.9 72.1 %all-reduce.5 = (f32[24]{0:T(128)}, f32[24]{0:T(128)}, f32[24]{0:T(128)}) all-reduce(f32[24]{0:T(128)S(1)} %get-tuple-element.1260, f32[24]{0:T(128)S(1)} %add.228, f32[24]{0:T(128)S(1)} %copy-done.28), channel_id=1, replica_groups=mesh['stream'=64,'seq'=2] {'stream','seq'}, use_global_device_ids=true, to_apply=%region_43.44 | all-reduce | flops 72 | bytes 576 | tf_op jit(solution)/shard_map/psum | solution.py:156
  (685 shorter events, 198.1 us)
Async XLA Ops:
  13.2 12.4 %copy-start.38 = (s32[64]{0:T(128)S(1)}, s32[64]{0:T(128)}, u32[]{:S(2)}) copy-start(s32[64]{0:T(128)} %param.29) | copy-start | bytes 772
  13.2 14.3 %copy-start.37 = (s32[1,2]{1,0:T(1,128)S(1)}, s32[1,2]{1,0:T(1,128)}, u32[]{:S(2)}) copy-start(s32[1,2]{1,0:T(1,128)} %param.30) | copy-start | bytes 28
  13.2 17.5 %copy-start.16 = (f32[1,24,1536]{2,1,0:T(8,128)S(1)}, f32[1,24,1536]{2,1,0:T(8,128)}, u32[]{:S(2)}) copy-start(f32[1,24,1536]{2,1,0:T(8,128)} %param.24) | copy-start | bytes 442372
  13.2 17.5 %copy-start.11 = (f32[24]{0:T(128)S(1)}, f32[24]{0:T(128)}, u32[]{:S(2)}) copy-start(f32[24]{0:T(128)} %param.26) | copy-start | bytes 292
  13.2 21.5 %copy-start.3 = (bf16[1,1536,256]{2,1,0:T(8,128)(2,1)S(1)}, bf16[1,1536,256]{2,1,0:T(8,128)(2,1)}, u32[]{:S(2)}) copy-start(bf16[1,1536,256]{2,1,0:T(8,128)(2,1)} %param.23) | copy-start | bytes 2359300
  13.2 458.0 %all-to-all-start = ((f32[64,1,12,64,128]{4,3,1,2,0:T(8,128)}), f32[64,1,12,64,128]{4,3,1,2,0:T(8,128)}, u32[]{:S(2)}, u32[]{:S(2)}) async-start(f32[64,1,12,64,128]{4,3,1,2,0:T(8,128)} %stack.2), calls=%async_computation | async-start | bytes 50331648 | tf_op jit(solution)/shard_map/all_to_all | solution.py:105
  30.9 28.7 %copy-start.1 = (f32[6,24,256]{2,1,0:T(8,128)}, f32[6,24,256]{2,1,0:T(8,128)S(1)}, u32[]{:S(2)}) copy-start(f32[6,24,256]{2,1,0:T(8,128)S(1)} %get-tuple-element.1772) | copy-start | bytes 442372
  34.6 25.0 %copy-start.12 = (f32[6,24,2]{1,2,0:T(2,128)}, f32[6,24,2]{1,2,0:T(2,128)S(1)}, u32[]{:S(2)}) copy-start(f32[6,24,2]{1,2,0:T(2,128)S(1)} %slice.164) | copy-start | bytes 3460
  35.0 24.8 %copy-start.7 = (f32[6,256,128]{1,2,0:T(8,128)}, f32[6,256,128]{1,2,0:T(8,128)S(1)}, u32[]{:S(2)}) copy-start(f32[6,256,128]{1,2,0:T(8,128)S(1)} %copy.260) | copy-start | bytes 2359300
  59.1 8.8 copy-start.14
  59.6 8.2 copy-start.21
  59.8 8.0 copy-start.17
  477.3 4.4 collective-permute-start
  520.0 6.4 copy-start.6
  520.1 6.2 copy-start
  532.1 7.0 copy-start.9
  532.1 7.0 copy-start.20
  532.1 8.0 copy-start.23
  532.1 8.0 copy-start.29
  552.6 6.4 copy-start.6
  552.8 6.2 copy-start
  564.7 7.0 copy-start.9
  564.7 7.0 copy-start.20
  564.7 8.0 copy-start.23
  564.8 8.0 copy-start.29
  585.2 6.4 copy-start.6
  597.4 7.0 copy-start.9
  597.4 7.0 copy-start.20
  597.4 8.0 copy-start.23
  597.4 8.0 copy-start.29
  617.8 6.4 copy-start.6
  618.0 6.2 copy-start
  630.0 7.0 copy-start.9
  630.0 7.0 copy-start.20
  630.0 8.0 copy-start.23
  630.0 8.0 copy-start.29
  650.4 6.4 copy-start.6
  650.6 6.2 copy-start
  662.6 7.0 copy-start.9
  662.6 7.0 copy-start.20
  662.6 8.0 copy-start.23
  662.6 8.0 copy-start.29
  683.1 6.4 copy-start.6
  683.3 6.2 copy-start
  695.2 7.0 copy-start.9
  695.2 7.0 copy-start.20
  695.2 8.0 copy-start.23
  695.3 8.0 copy-start.29
  704.5 11.6 %copy-start.36 = (f32[24]{0:T(128)S(1)}, f32[24]{0:T(128)}, u32[]{:S(2)}) copy-start(f32[24]{0:T(128)} %broadcast_multiply_fusion) | copy-start | bytes 292
  717.1 4.1 collective-permute-start.1
  721.2 15.2 %copy-start.15 = (f32[6,24]{1,0:T(8,128)S(1)}, f32[6,24]{1,0:T(8,128)}, u32[]{:S(2)}) copy-start(f32[6,24]{1,0:T(8,128)} %copy-done.14) | copy-start | bytes 1732
  721.2 15.2 %copy-start.33 = (pred[6]{0:T(512)(128)(4,1)S(1)}, pred[6]{0:T(512)(128)(4,1)}, u32[]{:S(2)}) copy-start(pred[6]{0:T(512)(128)(4,1)} %copy-done.32) | copy-start | bytes 22
  721.2 16.6 %copy-start.18 = (f32[6,24,256]{2,1,0:T(8,128)S(1)}, f32[6,24,256]{2,1,0:T(8,128)}, u32[]{:S(2)}) copy-start(f32[6,24,256]{2,1,0:T(8,128)} %copy-done.17) | copy-start | bytes 442372
  737.8 7.1 copy-start.2
  737.8 7.1 copy-start.13
  737.8 7.1 copy-start.22
  737.8 23.0 %copy-start.35 = (f32[24]{0:T(128)S(1)}, f32[24]{0:T(128)}, u32[]{:S(2)}) copy-start(f32[24]{0:T(128)} %copy-done.34) | copy-start | bytes 292
  737.8 23.4 %copy-start.10 = (f32[6,24,256]{2,1,0:T(8,128)S(1)}, f32[6,24,256]{2,1,0:T(8,128)}, u32[]{:S(2)}) copy-start(f32[6,24,256]{2,1,0:T(8,128)} %get-tuple-element.772) | copy-start | bytes 442372
  737.9 24.2 %copy-start.4 = (bf16[6,256,256]{1,2,0:T(8,128)(2,1)S(1)}, bf16[6,256,256]{1,2,0:T(8,128)(2,1)}, u32[]{:S(2)}) copy-start(bf16[6,256,256]{1,2,0:T(8,128)(2,1)} %get-tuple-element.771) | copy-start | bytes 2359300
  744.9 18.4 %copy-start.8 = (f32[6,256,128]{1,2,0:T(8,128)S(1)}, f32[6,256,128]{1,2,0:T(8,128)}, u32[]{:S(2)}) copy-start(f32[6,256,128]{1,2,0:T(8,128)} %copy-done.7) | copy-start | bytes 2359300
  780.6 13.1 %copy-start.25 = (f32[24]{0:T(128)S(1)}, f32[24]{0:T(128)}, u32[]{:S(2)}) copy-start(f32[24]{0:T(128)} %get-tuple-element.774) | copy-start | bytes 292
  780.6 13.7 %copy-start.39 = (f32[24]{0:T(128)S(1)}, f32[24]{0:T(128)}, u32[]{:S(2)}) copy-start(f32[24]{0:T(128)} %get-tuple-element.1819) | copy-start | bytes 292
  794.3 62.6 %copy-start.31 = (f32[24]{0:T(128)S(1)}, f32[24]{0:T(128)}, u32[]{:S(2)}) copy-start(f32[24]{0:T(128)} %get-tuple-element.775) | copy-start | bytes 292
  794.3 62.6 %copy-start.28 = (f32[24]{0:T(128)S(1)}, f32[24]{0:T(128)}, u32[]{:S(2)}) copy-start(f32[24]{0:T(128)} %get-tuple-element.776) | copy-start | bytes 292
  (34 other events, 74.4 us)
